TPU v7x, 32 devices: a whole 2x2x4 slice. The times are simulated.
32 devices in a mesh: nodes: 16 (over z, y, x), rep: 2 (over core).
Axes of the slice: x: 2, y: 2, z: 4, core: 2. Of those that a mesh axis runs over, the one named last changes fastest.
Arguments:
- node_latent: bfloat16 [5120, 512], P(('nodes', 'rep')), may hold values from -6 to 6
- edge_saved: bfloat16 [40960, 512], P(('nodes', 'rep')), may hold values from -6 to 6
- node_cot: bfloat16 [5120, 512], P(('nodes', 'rep')), may hold values from -6 to 6
- edge_cot: bfloat16 [40960, 512], P(('nodes', 'rep')), may hold values from -6 to 6
- senders: int32 [40960], P(('nodes', 'rep')), may hold values from 0 to 447, as said below
- receivers: int32 [40960], P(('nodes', 'rep')), may hold values from 0 to 319
- ghost_rows: int32 [16, 16, 8], P('nodes'), may hold values from 0 to 319, as said below
- w_edge_in: bfloat16 [1536, 512], replicated, may hold values from -0.15625 to 0.15625
- w_edge_out: bfloat16 [512, 512], replicated, may hold values from -0.25 to 0.25
- edge_gain: float32 [512], replicated, may hold values from 0.5 to 2
- edge_offset: float32 [512], replicated, may hold values from -3 to 3
- w_node_in: bfloat16 [1024, 512], replicated, may hold values from -0.1875 to 0.1875
- w_node_out: bfloat16 [512, 512], replicated, may hold values from -0.25 to 0.25
- node_gain: float32 [512], replicated, may hold values from 0.5 to 2
Outputs:
- grad_nodes: bfloat16 [5120, 512], P(('nodes', 'rep'))
- grad_edges: bfloat16 [40960, 512], P(('nodes', 'rep'))
- grad_edge_in: bfloat16 [1536, 512], replicated
- grad_edge_out: bfloat16 [512, 512], replicated
- grad_node_in: bfloat16 [1024, 512], replicated
- grad_node_out: bfloat16 [512, 512], replicated
Inputs may be any that keep to these rules, and one draw needn't show every extreme that they name: `senders`: A sender below 320 is a node of the edge's own partition; otherwise it is 320 + q * 8 + s, the ghost slot s of the list of a partition q other than the edge's own. Each list ghost_rows[q, p] holds 8 distinct rows.
All inputs are finite; a program needn't handle non-finite values.
Results may differ from a plain program's by a relative error of at most 0.008.
Values may be sent and summed in bfloat16 or wider, within the bound.
A program may use at most 128 MiB of HBM per device.

v0:
```python
import math
import jax
import jax.numpy as jnp
from jax import lax
from jax.sharding import PartitionSpec as P

EPS = 1e-05


def swapped(array, axis, bit):
    return lax.ppermute(array, axis, [(i, i ^ 1 << bit) for i in range(lax.axis_size(axis))])


def mat_mul(left, right):
    return jnp.dot(left, right, preferred_element_type=jnp.float32)


def mat_tn(left, right):
    return lax.dot_general(
        left, right, (((0,), (0,)), ((), ())), preferred_element_type=jnp.float32
    )


def mat_nt(left, right):
    return lax.dot_general(
        left, right, (((1,), (1,)), ((), ())), preferred_element_type=jnp.float32
    )


def silu_slope(value):
    sigmoid_v = jax.nn.sigmoid(value)
    return sigmoid_v * (1.0 + value * (1.0 - sigmoid_v))


def norm_forward(value):
    centred = value - jnp.mean(value, axis=-1, keepdims=True)
    inverse = lax.rsqrt(jnp.mean(centred * centred, axis=-1, keepdims=True) + EPS)
    return (centred * inverse, inverse)


def norm_backward(grad_hat, normed, inverse):
    return inverse * (
        grad_hat
        - jnp.mean(grad_hat, axis=-1, keepdims=True)
        - normed * jnp.mean(grad_hat * normed, axis=-1, keepdims=True)
    )


def edge_forward(edge_block, send_rows, recv_rows, w_edge_in, w_edge_out, edge_gain, edge_offset):
    latent_width = edge_block.shape[1]
    pre_act = (
        mat_mul(edge_block, w_edge_in[:latent_width])
        + mat_mul(send_rows, w_edge_in[latent_width : 2 * latent_width])
        + mat_mul(recv_rows, w_edge_in[2 * latent_width :])
    )
    edge_hidden = jax.nn.silu(pre_act).astype(jnp.bfloat16)
    edge_normed, edge_inverse = norm_forward(mat_mul(edge_hidden, w_edge_out))
    message = edge_normed * edge_gain + edge_offset
    return (pre_act, edge_hidden, edge_normed, edge_inverse, message)


def edge_backward(
    edge_block,
    send_rows,
    recv_rows,
    edge_cot,
    message_grad,
    saved,
    w_edge_in,
    w_edge_out,
    edge_gain,
):
    pre_act, edge_hidden, edge_normed, edge_inverse = saved
    latent_width = edge_block.shape[1]
    grad_out = norm_backward(message_grad * edge_gain, edge_normed, edge_inverse).astype(
        jnp.bfloat16
    )
    grad_act = (mat_nt(grad_out, w_edge_out) * silu_slope(pre_act)).astype(jnp.bfloat16)
    in_grad = jnp.concatenate(
        [mat_tn(edge_block, grad_act), mat_tn(send_rows, grad_act), mat_tn(recv_rows, grad_act)], 0
    )
    out_grad = mat_tn(edge_hidden, grad_out)
    edge_grad = (edge_cot.astype(jnp.float32) + mat_nt(grad_act, w_edge_in[:latent_width])).astype(
        jnp.bfloat16
    )
    send_grad = mat_nt(grad_act, w_edge_in[latent_width : 2 * latent_width])
    recv_grad = mat_nt(grad_act, w_edge_in[2 * latent_width :])
    return (edge_grad, send_grad, recv_grad, in_grad, out_grad)


def node_pass(node_rows, totals_b, node_cot, w_node_in, w_node_out, node_gain):
    latent_width = node_rows.shape[1]
    node_pre = mat_mul(node_rows, w_node_in[:latent_width]) + mat_mul(
        totals_b, w_node_in[latent_width:]
    )
    node_hidden = jax.nn.silu(node_pre).astype(jnp.bfloat16)
    node_normed, node_inverse = norm_forward(mat_mul(node_hidden, w_node_out))
    grad_out = norm_backward(
        node_cot.astype(jnp.float32) * node_gain, node_normed, node_inverse
    ).astype(jnp.bfloat16)
    grad_act = (mat_nt(grad_out, w_node_out) * silu_slope(node_pre)).astype(jnp.bfloat16)
    in_grad = jnp.concatenate([mat_tn(node_rows, grad_act), mat_tn(totals_b, grad_act)], 0)
    direct_grad = mat_nt(grad_act, w_node_in[:latent_width])
    totals_grad = mat_nt(grad_act, w_node_in[latent_width:]).astype(jnp.bfloat16)
    return (direct_grad, totals_grad, in_grad, mat_tn(node_hidden, grad_out))


def shards(
    node_latent,
    edge_saved,
    node_cot,
    edge_cot,
    senders,
    receivers,
    ghost_rows,
    w_edge_in,
    w_edge_out,
    edge_gain,
    edge_offset,
    w_node_in,
    w_node_out,
    node_gain,
):
    latent_width = node_latent.shape[1]
    edge_latent = swapped(edge_saved, "rep", 0)
    partition = lax.all_gather(node_latent, "rep", axis=0, tiled=True)
    part_rows = partition.shape[0]
    ghost_lists = ghost_rows[0]
    part_count = ghost_lists.shape[0]
    slot_count = ghost_lists.shape[1]
    outgoing = partition[ghost_lists.reshape(-1)].reshape(part_count, slot_count, latent_width)
    ghosts = lax.all_to_all(outgoing, "nodes", split_axis=0, concat_axis=0, tiled=True)
    node_table = jnp.concatenate(
        [partition, ghosts.reshape(part_count * slot_count, latent_width)], 0
    )
    send_rows = node_table[senders]
    recv_rows = partition[receivers]
    pre_act, edge_hidden, edge_normed, edge_inverse, message = edge_forward(
        edge_latent, send_rows, recv_rows, w_edge_in, w_edge_out, edge_gain, edge_offset
    )
    partial_totals = jax.ops.segment_sum(message, receivers, num_segments=part_rows)
    totals = lax.psum_scatter(partial_totals, "rep", scatter_dimension=0, tiled=True)
    direct_grad, totals_grad, node_in_grad, node_out_grad = node_pass(
        node_latent, totals.astype(jnp.bfloat16), node_cot, w_node_in, w_node_out, node_gain
    )
    partition_totals_grad = lax.all_gather(totals_grad, "rep", axis=0, tiled=True)
    message_grad = edge_cot.astype(jnp.float32) + partition_totals_grad[receivers].astype(
        jnp.float32
    )
    edge_grad, send_grad, recv_grad, edge_in_grad, edge_out_grad = edge_backward(
        edge_latent,
        send_rows,
        recv_rows,
        edge_cot,
        message_grad,
        (pre_act, edge_hidden, edge_normed, edge_inverse),
        w_edge_in,
        w_edge_out,
        edge_gain,
    )
    table_grad = jax.ops.segment_sum(send_grad, senders, num_segments=node_table.shape[0])
    row_grad = table_grad[:part_rows] + jax.ops.segment_sum(
        recv_grad, receivers, num_segments=part_rows
    )
    ghost_grad = table_grad[part_rows:].reshape(part_count, slot_count, latent_width)
    returned = lax.all_to_all(
        ghost_grad.astype(jnp.bfloat16), "nodes", split_axis=0, concat_axis=0, tiled=True
    ).astype(ghost_grad.dtype)
    row_grad = row_grad + jax.ops.segment_sum(
        returned.reshape(-1, latent_width), ghost_lists.reshape(-1), num_segments=part_rows
    )
    own_grad = lax.psum_scatter(row_grad, "rep", scatter_dimension=0, tiled=True)
    grad_nodes = (own_grad + direct_grad + node_cot.astype(jnp.float32)).astype(jnp.bfloat16)
    weight_grads = (edge_in_grad, edge_out_grad, node_in_grad, node_out_grad)
    device_count = lax.axis_size("nodes") * lax.axis_size("rep")
    edge_scale = 1.0 / math.sqrt(senders.shape[0] * device_count)
    node_scale = 1.0 / math.sqrt(node_latent.shape[0] * device_count)
    weight_total = lax.psum(
        (weight_grads[0], weight_grads[1], weight_grads[2], weight_grads[3]), ("nodes", "rep")
    )
    return (
        grad_nodes,
        edge_grad,
        (weight_total[0] * edge_scale).astype(jnp.bfloat16),
        (weight_total[1] * edge_scale).astype(jnp.bfloat16),
        (weight_total[2] * node_scale).astype(jnp.bfloat16),
        (weight_total[3] * node_scale).astype(jnp.bfloat16),
    )


def solution(mesh):
    return jax.shard_map(
        shards,
        mesh=mesh,
        in_specs=(
            P(("nodes", "rep"), None),
            P(("nodes", "rep"), None),
            P(("nodes", "rep"), None),
            P(("nodes", "rep"), None),
            P(("nodes", "rep")),
            P(("nodes", "rep")),
            P("nodes", None, None),
            P(),
            P(),
            P(),
            P(),
            P(),
            P(),
            P(),
        ),
        out_specs=(P(("nodes", "rep"), None), P(("nodes", "rep"), None), P(), P(), P(), P()),
        check_vma=False,
    )
```

profile of v0, /device:TPU:0, one launch (start us, length us, event | category | flops | bytes accessed | tf_op | source)
XLA Modules:
  0.0 329.2 jit_solution(6399339282677917739)
XLA Ops:
  7.2 2.5 all_gather.6
  12.1 8.2 %all-to-all-start = ((bf16[16,8,512]{2,1,0:T(8,128)(2,1)}), bf16[16,8,512]{2,1,0:T(8,128)(2,1)S(1)}, u32[]{:S(2)}, u32[]{:S(2)}) async-start(bf16[16,8,512]{2,1,0:T(8,128)(2,1)} %bitcast.1), calls=%async_computation | async-start | bytes 262144 | tf_op jit(solution)/shard_map/all_to_all | solution.py:132
  21.1 4.1 %gather_fusion.2 = bf16[1280,512]{1,0:T(8,128)(2,1)S(1)} fusion(bf16[320,512]{1,0:T(8,128)(2,1)S(1)} %all_gather.6, s32[2048]{0:T(1024)S(1)} %pad_clamp_fusion), kind=kCustom, calls=%fused_computation.2 | custom fusion | bytes 2626560 | tf_op jit(solution)/shard_map/gather | solution.py:137
  25.3 3.8 %fusion.15 = f32[1280,512]{1,0:T(8,128)} fusion(bf16[1280,512]{1,0:T(8,128)(2,1)S(1)} %gather_fusion.2, bf16[1536,512]{1,0:T(8,128)(2,1)} %param.21), kind=kOutput, calls=%fused_computation.46 | convolution fusion | flops 671088640 | bytes 4456448 | tf_op jit(solution)/shard_map/dot_general | solution.py:15
  29.1 4.1 %gather_fusion.1 = bf16[1280,512]{1,0:T(8,128)(2,1)S(1)} fusion(bf16[448,512]{1,0:T(8,128)(2,1)S(1)} %pad_maximum_fusion.2, s32[2048]{0:T(1024)S(1)} %pad_clamp_fusion.1), kind=kCustom, calls=%fused_computation.1 | custom fusion | bytes 2626560 | tf_op jit(solution)/shard_map/gather | solution.py:136
  33.2 2.4 fusion.19
  35.7 4.2 %multiply_convert_fusion.2 = (bf16[1280,512]{1,0:T(8,128)(2,1)S(1)}, f32[1280,512]{1,0:T(8,128)}) fusion(f32[1280,512]{1,0:T(8,128)S(1)} %copy-done.12, f32[1280,512]{1,0:T(8,128)S(1)} %fusion.19, bf16[1280,512]{1,0:T(8,128)(2,1)} %collective-permute-done, bf16[1536,512]{1,0:T(8,128)(2,1)} %param.21), kind=kOutput, calls=%fused_computation.22 | convolution fusion | flops 675676160 | bytes 11010048 | tf_op jit(solution)/shard_map/dot_general | solution.py:15
  43.6 3.2 copy.28
  46.9 11.1 %scatter_custom_fusion = f32[320,512]{1,0:T(8,128)} fusion(s32[1280]{0:T(1024)S(1)} %copy-done.34, f32[1280,512]{1,0:T(8,128)} %copy.28, f32[]{:T(128)} %constant.10.clone.1), kind=kCustom, calls=%fused_computation.70 | custom fusion | flops 655360 | bytes 655872 | tf_op jit(solution)/shard_map/scatter-add | solution.py:141
  58.1 2.4 copy.27
  62.5 5.1 %reduce-scatter.3.cloned.1.call-done = f32[160,512]{1,0:T(8,128)} async-done(((f32[320,512]{1,0:T(8,128)}), f32[160,512]{1,0:T(8,128)}) %reduce-scatter.3.cloned.1.call-update) | async-done | bytes 327696 | tf_op jit(solution)/shard_map/reduce_scatter | solution.py:142
  74.9 4.7 %gather_fusion.3 = bf16[1280,512]{1,0:T(8,128)(2,1)} fusion(bf16[320,512]{1,0:T(8,128)(2,1)S(1)} %all_gather.7, s32[2048]{0:T(1024)S(1)} %pad_clamp_fusion), kind=kCustom, calls=%fused_computation.3 | custom fusion | bytes 2626560 | tf_op jit(solution)/shard_map/gather | solution.py:147
  79.6 2.4 copy.29
  82.1 2.7 fusion.4
  88.0 2.4 fusion.17
  92.8 10.6 %scatter_custom_fusion.1 = f32[448,512]{1,0:T(8,128)S(1)} fusion(s32[1280]{0:T(1024)S(1)} %copy-done.36, f32[1280,512]{1,0:T(8,128)} %fusion.17, f32[]{:T(128)} %constant.10.clone.1), kind=kCustom, calls=%fused_computation.55 | custom fusion | flops 655360 | bytes 918016 | tf_op jit(solution)/shard_map/scatter-add | solution.py:161
  104.1 3.2 fusion.50
  108.8 6.7 %all-to-all-start.1 = ((bf16[16,8,512]{2,1,0:T(8,128)(2,1)}), bf16[16,8,512]{2,1,0:T(8,128)(2,1)S(1)}, u32[]{:S(2)}, u32[]{:S(2)}) async-start(bf16[16,8,512]{2,1,0:T(8,128)(2,1)} %fusion.37), calls=%async_computation.2 | async-start | bytes 262144 | tf_op jit(solution)/shard_map/all_to_all | solution.py:166
  115.7 10.7 %scatter_fusion = f32[320,512]{1,0:T(8,128)S(1)} fusion(f32[320,512]{1,0:T(8,128)S(1)} %slice.42, s32[1280]{0:T(1024)S(1)} %copy-done.34, f32[1280,512]{1,0:T(8,128)} %fusion.13), kind=kCustom, calls=%fused_computation.6 | custom fusion | flops 655360 | bytes 7869440 | tf_op jit(solution)/shard_map/scatter-add | solution.py:162
  131.7 3.2 pad_maximum_fusion.1
  144.1 3.0 fusion.1
  147.1 2.5 copy.32
  151.6 164.3 %all-reduce.3.cloned.1.call-done = (f32[1536,512]{1,0:T(8,128)}, f32[512,512]{1,0:T(8,128)}, f32[1024,512]{1,0:T(8,128)}, f32[512,512]{1,0:T(8,128)}) async-done(((f32[1536,512]{1,0:T(8,128)}, f32[512,512]{1,0:T(8,128)}, f32[1024,512]{1,0:T(8,128)}, f32[512,512]{1,0:T(8,128)}), (f32[1536,512]{1,0:T(8,128)}, f32[512,512]{1,0:T(8,128)}, f32[1024,512]{1,0:T(8,128)}, ...) | async-done | bytes 7340048 | tf_op jit(solution)/shard_map/psum | solution.py:178
  315.9 3.6 %multiply_convert_fusion = bf16[1536,512]{1,0:T(8,128)(2,1)} fusion(f32[1536,512]{1,0:T(8,128)} %get-tuple-element.22), kind=kLoop, calls=%fused_computation.14 | loop fusion | flops 1572864 | bytes 4718592 | tf_op jit(solution)/shard_map/convert_element_type | solution.py:184
  (140 shorter events, 43.7 us)
Async XLA Ops:
  7.2 32.7 %copy-start = (bf16[512,512]{1,0:T(8,128)(2,1)S(1)}, bf16[512,512]{1,0:T(8,128)(2,1)}, u32[]{:S(2)}) copy-start(bf16[512,512]{1,0:T(8,128)(2,1)} %param.22) | copy-start | bytes 1572868
  12.1 17.0 %all-to-all-start = ((bf16[16,8,512]{2,1,0:T(8,128)(2,1)}), bf16[16,8,512]{2,1,0:T(8,128)(2,1)S(1)}, u32[]{:S(2)}, u32[]{:S(2)}) async-start(bf16[16,8,512]{2,1,0:T(8,128)(2,1)} %bitcast.1), calls=%async_computation | async-start | bytes 262144 | tf_op jit(solution)/shard_map/all_to_all | solution.py:132
  20.3 47.3 %reduce-scatter.3.cloned.1.call-start = ((), (), s32[]{:S(2)}) async-start(), calls=%async_computation.4 | async-start | bytes 983040 | tf_op jit(solution)/shard_map/reduce_scatter | solution.py:142
  20.3 15.3 %collective-permute-start = (bf16[1280,512]{1,0:T(8,128)(2,1)}, bf16[1280,512]{1,0:T(8,128)(2,1)}, u32[]{:S(2)}, u32[]{:S(2)}) collective-permute-start(bf16[1280,512]{1,0:T(8,128)(2,1)} %param.15), channel_id=1, source_target_pairs={{0,1},{1,0},{2,3},{3,2},{4,5},{5,4},{6,7},{7,6},{8,9},{9,8},{10,11... | collective-permute-start | bytes 3932168 | tf_op jit(solution)/shard_map/ppermute | solution.py:11
  21.1 4.1 %copy-start.36 = (s32[1280]{0:T(1024)S(1)}, s32[1280]{0:T(1024)}, u32[]{:S(2)}) copy-start(s32[1280]{0:T(1024)} %param.18) | copy-start | bytes 15364
  25.3 3.8 %copy-start.7 = (bf16[1280,512]{1,0:T(8,128)(2,1)}, bf16[1280,512]{1,0:T(8,128)(2,1)S(1)}, u32[]{:S(2)}) copy-start(bf16[1280,512]{1,0:T(8,128)(2,1)S(1)} %gather_fusion.2) | copy-start | bytes 3932164
  46.8 13.6 %copy-start.16 = (bf16[160,512]{1,0:T(8,128)(2,1)S(1)}, bf16[160,512]{1,0:T(8,128)(2,1)}, u32[]{:S(2)}) copy-start(bf16[160,512]{1,0:T(8,128)(2,1)} %param.14) | copy-start | bytes 491524
  62.5 8.4 %copy-start.30 = (bf16[160,512]{1,0:T(8,128)(2,1)S(1)}, bf16[160,512]{1,0:T(8,128)(2,1)}, u32[]{:S(2)}) copy-start(bf16[160,512]{1,0:T(8,128)(2,1)} %param.16) | copy-start | bytes 491524
  62.5 8.4 %copy-start.38 = (f32[512]{0:T(512)S(1)}, f32[512]{0:T(512)}, u32[]{:S(2)}) copy-start(f32[512]{0:T(512)} %param.27) | copy-start | bytes 6148
  67.6 3.6 %copy-start.39 = (bf16[512,512]{1,0:T(8,128)(2,1)S(1)}, bf16[512,512]{1,0:T(8,128)(2,1)}, u32[]{:S(2)}) copy-start(bf16[512,512]{1,0:T(8,128)(2,1)} %param.26) | copy-start | bytes 1572868
  92.8 11.3 %copy-start.8 = (bf16[1280,512]{1,0:T(8,128)(2,1)S(1)}, bf16[1280,512]{1,0:T(8,128)(2,1)}, u32[]{:S(2)}) copy-start(bf16[1280,512]{1,0:T(8,128)(2,1)} %copy-done.7) | copy-start | bytes 3932164
  104.1 3.2 copy-start.21
  104.1 3.2 copy-start.31
  104.1 3.2 copy-start.33
  108.8 20.3 %all-to-all-start.1 = ((bf16[16,8,512]{2,1,0:T(8,128)(2,1)}), bf16[16,8,512]{2,1,0:T(8,128)(2,1)S(1)}, u32[]{:S(2)}, u32[]{:S(2)}) async-start(bf16[16,8,512]{2,1,0:T(8,128)(2,1)} %fusion.37), calls=%async_computation.2 | async-start | bytes 262144 | tf_op jit(solution)/shard_map/all_to_all | solution.py:166
  115.6 10.8 %copy-start.19 = (bf16[160,512]{1,0:T(8,128)(2,1)S(1)}, bf16[160,512]{1,0:T(8,128)(2,1)}, u32[]{:S(2)}) copy-start(bf16[160,512]{1,0:T(8,128)(2,1)} %copy-done.18) | copy-start | bytes 491524
  115.6 10.8 %copy-start.26 = (f32[160,512]{1,0:T(8,128)S(1)}, f32[160,512]{1,0:T(8,128)}, u32[]{:S(2)}) copy-start(f32[160,512]{1,0:T(8,128)} %reduce-scatter.3.cloned.1.call-done) | copy-start | bytes 983044
  115.6 12.2 %copy-start.17 = (bf16[160,512]{1,0:T(8,128)(2,1)S(1)}, bf16[160,512]{1,0:T(8,128)(2,1)}, u32[]{:S(2)}) copy-start(bf16[160,512]{1,0:T(8,128)(2,1)} %param.14) | copy-start | bytes 491524
  115.6 34.0 %reduce-scatter.5.cloned.1.call-start = ((), (), s32[]{:S(2)}) async-start(), calls=%async_computation.5 | async-start | bytes 983040 | tf_op jit(solution)/shard_map/reduce_scatter | solution.py:172
  131.6 3.3 %copy-start.6 = (bf16[1280,512]{1,0:T(8,128)(2,1)S(1)}, bf16[1280,512]{1,0:T(8,128)(2,1)}, u32[]{:S(2)}) copy-start(bf16[1280,512]{1,0:T(8,128)(2,1)} %copy-done.5) | copy-start | bytes 3932164
  131.6 3.3 copy-start.10
  131.6 184.3 %all-reduce.3.cloned.1.call-start = ((), (), s32[]{:S(2)}) async-start(), calls=%async_computation.6 | async-start | bytes 14680064 | tf_op jit(solution)/shard_map/psum | solution.py:178
  315.9 3.6 %copy-start.28 = (f32[512,512]{1,0:T(8,128)S(1)}, f32[512,512]{1,0:T(8,128)}, u32[]{:S(2)}) copy-start(f32[512,512]{1,0:T(8,128)} %get-tuple-element.23) | copy-start | bytes 3145732
  315.9 4.6 %copy-start.15 = (f32[1024,512]{1,0:T(8,128)S(1)}, f32[1024,512]{1,0:T(8,128)}, u32[]{:S(2)}) copy-start(f32[1024,512]{1,0:T(8,128)} %get-tuple-element.24) | copy-start | bytes 6291460
  (23 other events, 43.6 us)
Sparse Core Ops, SparseCore 0:
  58.1 9.4 reduce-scatter.2
  131.7 9.3 reduce-scatter.4
  147.3 168.5 all-reduce.2
where the time goes:
time: 330 us; the launch traced here: 329 us
  waiting for transfers between devices  169 us (51%)
  other arithmetic  53.9 us (16%)
  matrix products  40.7 us (12%)
  local copies, waits for them, and re-layouts  31 us (9%)
  starting transfers between devices  15.1 us (5%)
  between operations  14.3 us (4%)
  blocking collectives  4.72 us (1%)
    psum x1, waiting for transfers between devices, shards(): lax.psum((weight_grads[0], weight_grads[1], weight_grads[2], weight_grads...  164 us
    dot_general x7, matrix products, mat_mul(): return jnp.dot(left, right, preferred_element_type=jnp.float32)  16.4 us
    dot_general x7, matrix products, mat_tn(): lax.dot_general(left, right, (((0,), (0,)), ((), ())), preferred_element_...  12.4 us
    dot_general x7, matrix products, mat_nt(): lax.dot_general(left, right, (((1,), (1,)), ((), ())), preferred_element_...  11.9 us
    scatter-add x1, other arithmetic, shards(): jax.ops.segment_sum(message, receivers, num_segments=part_rows)  11.1 us
    scatter-add x1, other arithmetic, shards(): jax.ops.segment_sum(recv_grad, receivers, num_segments=part_rows)  10.7 us
    scatter-add x1, other arithmetic, shards(): jax.ops.segment_sum(send_grad, senders, num_segments=node_table.shape[0])  10.6 us
    unnamed x85, local copies, waits for them, and re-layouts  10.1 us
  transfers between devices with their start and end apart: 6, of which 2 were waited for; matrix products, arithmetic and copies ran while one was open for 15% of the time, Pallas kernels for 0%

commit v1 on v0

--- a/solution.py
+++ b/solution.py
@@ -176,7 +176,8 @@
     edge_scale = 1.0 / math.sqrt(senders.shape[0] * device_count)
     node_scale = 1.0 / math.sqrt(node_latent.shape[0] * device_count)
     weight_total = lax.psum(
-        (weight_grads[0], weight_grads[1], weight_grads[2], weight_grads[3]), ("nodes", "rep")
+        lax.psum((weight_grads[0], weight_grads[1], weight_grads[2], weight_grads[3]), "nodes"),
+        "rep",
     )
     return (
         grad_nodes,

time: 330 us -> 399 us (1.21)
  waiting for transfers between devices: 169 us -> 239 us
    psum x0 -> x1, waiting for transfers between devices: none -> 36.3 us  [shards(): lax.psum(lax.psum((weight_grads[0], weight_grads[1], weight_grads[2], wei...]
    psum x1, waiting for transfers between devices: 164 us -> 195 us  [shards(): lax.psum((weight_grads[0], weight_grads[1], weight_grads[2], weight_grads...]
    dot_general x7, matrix products: 12.4 us -> 7.91 us  [mat_tn(): lax.dot_general(left, right, (((0,), (0,)), ((), ())), preferred_element_...]
    unnamed x85 -> x73, local copies, waits for them, and re-layouts: 10.1 us -> 10.2 us
  transfers between devices with their start and end apart: 6 -> 7, of which waited for: 2 -> 4; matrix products, arithmetic and copies ran while one was open for 15% -> 15% of each run, Pallas kernels for 0% -> 0%
where the time goes in v1:
time: 399 us; the launch traced here: 398 us
  waiting for transfers between devices  239 us (60%)
  other arithmetic  53 us (13%)
  matrix products  38.2 us (10%)
  local copies, waits for them, and re-layouts  33.2 us (8%)
  starting transfers between devices  15.2 us (4%)
  between operations  14.2 us (4%)
  blocking collectives  4.72 us (1%)
    psum x1, waiting for transfers between devices, shards(): lax.psum((weight_grads[0], weight_grads[1], weight_grads[2], weight_grads...  195 us
    psum x1, waiting for transfers between devices, shards(): lax.psum(lax.psum((weight_grads[0], weight_grads[1], weight_grads[2], wei...  36.3 us
    dot_general x7, matrix products, mat_mul(): return jnp.dot(left, right, preferred_element_type=jnp.float32)  16.4 us
    dot_general x7, matrix products, mat_nt(): lax.dot_general(left, right, (((1,), (1,)), ((), ())), preferred_element_...  13.9 us
    scatter-add x1, other arithmetic, shards(): jax.ops.segment_sum(send_grad, senders, num_segments=node_table.shape[0])  11.4 us
    scatter-add x1, other arithmetic, shards(): jax.ops.segment_sum(message, receivers, num_segments=part_rows)  11.1 us
    scatter-add x1, other arithmetic, shards(): jax.ops.segment_sum(recv_grad, receivers, num_segments=part_rows)  10.6 us
    unnamed x73, local copies, waits for them, and re-layouts  10.2 us
  transfers between devices with their start and end apart: 7, of which 4 were waited for; matrix products, arithmetic and copies ran while one was open for 15% of the time, Pallas kernels for 0%

profile of v1, /device:TPU:0, one launch (start us, length us, event | category | flops | bytes accessed | tf_op | source)
XLA Modules:
  0.0 398.0 jit_solution(6100553544853896985)
XLA Ops:
  7.2 2.5 all_gather.6
  12.1 8.2 %all-to-all-start = ((bf16[16,8,512]{2,1,0:T(8,128)(2,1)}), bf16[16,8,512]{2,1,0:T(8,128)(2,1)S(1)}, u32[]{:S(2)}, u32[]{:S(2)}) async-start(bf16[16,8,512]{2,1,0:T(8,128)(2,1)} %bitcast.1), calls=%async_computation | async-start | bytes 262144 | tf_op jit(solution)/shard_map/all_to_all | solution.py:132
  21.1 4.1 %gather_fusion.2 = bf16[1280,512]{1,0:T(8,128)(2,1)S(1)} fusion(bf16[320,512]{1,0:T(8,128)(2,1)S(1)} %all_gather.6, s32[2048]{0:T(1024)S(1)} %pad_clamp_fusion), kind=kCustom, calls=%fused_computation.2 | custom fusion | bytes 2626560 | tf_op jit(solution)/shard_map/gather | solution.py:137
  25.3 3.7 fusion.15
  29.1 4.1 %gather_fusion.1 = bf16[1280,512]{1,0:T(8,128)(2,1)S(1)} fusion(bf16[448,512]{1,0:T(8,128)(2,1)S(1)} %pad_maximum_fusion.2, s32[2048]{0:T(1024)S(1)} %pad_clamp_fusion.1), kind=kCustom, calls=%fused_computation.1 | custom fusion | bytes 2626560 | tf_op jit(solution)/shard_map/gather | solution.py:136
  35.6 4.3 %multiply_convert_fusion.2 = (bf16[1280,512]{1,0:T(8,128)(2,1)S(1)}, f32[1280,512]{1,0:T(8,128)}) fusion(f32[1280,512]{1,0:T(8,128)S(1)} %copy-done.9, f32[1280,512]{1,0:T(8,128)S(1)} %fusion.19, bf16[1280,512]{1,0:T(8,128)(2,1)} %collective-permute-done, bf16[1536,512]{1,0:T(8,128)(2,1)} %param.21), kind=kOutput, calls=%fused_computation.22 | convolution fusion | flops 675676160 | bytes 11010048 | tf_op jit(solution)/shard_map/dot_general | solution.py:15
  43.6 3.3 copy.28
  47.0 11.1 %scatter_custom_fusion = f32[320,512]{1,0:T(8,128)} fusion(s32[1280]{0:T(1024)S(1)} %copy-done.28, f32[1280,512]{1,0:T(8,128)} %copy.28, f32[]{:T(128)} %constant.10.clone.1), kind=kCustom, calls=%fused_computation.70 | custom fusion | flops 655360 | bytes 655872 | tf_op jit(solution)/shard_map/scatter-add | solution.py:141
  58.1 2.4 copy.27
  62.6 5.1 %reduce-scatter.3.cloned.1.call-done = f32[160,512]{1,0:T(8,128)} async-done(((f32[320,512]{1,0:T(8,128)}), f32[160,512]{1,0:T(8,128)}) %reduce-scatter.3.cloned.1.call-update) | async-done | bytes 327696 | tf_op jit(solution)/shard_map/reduce_scatter | solution.py:142
  75.0 4.7 %gather_fusion.3 = bf16[1280,512]{1,0:T(8,128)(2,1)} fusion(bf16[320,512]{1,0:T(8,128)(2,1)S(1)} %all_gather.7, s32[2048]{0:T(1024)S(1)} %pad_clamp_fusion), kind=kCustom, calls=%fused_computation.3 | custom fusion | bytes 2626560 | tf_op jit(solution)/shard_map/gather | solution.py:147
  79.7 2.4 copy.29
  82.2 2.7 fusion.4
  100.7 3.4 fusion.17
  104.2 11.4 %scatter_custom_fusion.1 = f32[448,512]{1,0:T(8,128)} fusion(s32[1280]{0:T(1024)S(1)} %copy-done.30, f32[1280,512]{1,0:T(8,128)} %fusion.17, f32[]{:T(128)} %constant.10.clone.1), kind=kCustom, calls=%fused_computation.55 | custom fusion | flops 655360 | bytes 918016 | tf_op jit(solution)/shard_map/scatter-add | solution.py:161
  118.3 6.7 %all-to-all-start.1 = ((bf16[16,8,512]{2,1,0:T(8,128)(2,1)}), bf16[16,8,512]{2,1,0:T(8,128)(2,1)S(1)}, u32[]{:S(2)}, u32[]{:S(2)}) async-start(bf16[16,8,512]{2,1,0:T(8,128)(2,1)} %fusion.37), calls=%async_computation.2 | async-start | bytes 262144 | tf_op jit(solution)/shard_map/all_to_all | solution.py:166
  125.1 3.4 fusion.13
  128.5 10.6 %scatter_fusion = f32[320,512]{1,0:T(8,128)S(1)} fusion(f32[320,512]{1,0:T(8,128)S(1)} %slice.42, s32[1280]{0:T(1024)S(1)} %copy-done.28, f32[1280,512]{1,0:T(8,128)} %fusion.13), kind=kCustom, calls=%fused_computation.6 | custom fusion | flops 655360 | bytes 7869440 | tf_op jit(solution)/shard_map/scatter-add | solution.py:162
  141.7 195.5 %all-reduce.5.cloned.1.call-done = (f32[1536,512]{1,0:T(8,128)}, f32[512,512]{1,0:T(8,128)}, f32[1024,512]{1,0:T(8,128)}, f32[512,512]{1,0:T(8,128)}) async-done(((f32[1536,512]{1,0:T(8,128)}, f32[512,512]{1,0:T(8,128)}, f32[1024,512]{1,0:T(8,128)}, f32[512,512]{1,0:T(8,128)}), (f32[1536,512]{1,0:T(8,128)}, f32[512,512]{1,0:T(8,128)}, f32[1024,512]{1,0:T(8,128)}, ...) | async-done | bytes 7340048 | tf_op jit(solution)/shard_map/psum | solution.py:179
  338.5 3.0 fusion.1
  341.5 2.5 copy.32
  344.0 2.5 reduce-scatter.5.cloned.1.call-done
  348.4 36.3 %all-reduce.7.cloned.1.call-done = (f32[1536,512]{1,0:T(8,128)}, f32[512,512]{1,0:T(8,128)}, f32[1024,512]{1,0:T(8,128)}, f32[512,512]{1,0:T(8,128)}) async-done(((f32[1536,512]{1,0:T(8,128)}, f32[512,512]{1,0:T(8,128)}, f32[1024,512]{1,0:T(8,128)}, f32[512,512]{1,0:T(8,128)}), (f32[1536,512]{1,0:T(8,128)}, f32[512,512]{1,0:T(8,128)}, f32[1024,512]{1,0:T(8,128)}, ...) | async-done | bytes 7340048 | tf_op jit(solution)/shard_map/psum | solution.py:178
  384.7 3.6 multiply_convert_fusion
  (131 shorter events, 46.2 us)
Async XLA Ops:
  7.2 32.8 %copy-start = (bf16[512,512]{1,0:T(8,128)(2,1)S(1)}, bf16[512,512]{1,0:T(8,128)(2,1)}, u32[]{:S(2)}) copy-start(bf16[512,512]{1,0:T(8,128)(2,1)} %param.22) | copy-start | bytes 1572868
  12.1 17.0 %all-to-all-start = ((bf16[16,8,512]{2,1,0:T(8,128)(2,1)}), bf16[16,8,512]{2,1,0:T(8,128)(2,1)S(1)}, u32[]{:S(2)}, u32[]{:S(2)}) async-start(bf16[16,8,512]{2,1,0:T(8,128)(2,1)} %bitcast.1), calls=%async_computation | async-start | bytes 262144 | tf_op jit(solution)/shard_map/all_to_all | solution.py:132
  20.3 47.4 %reduce-scatter.3.cloned.1.call-start = ((), (), s32[]{:S(2)}) async-start(), calls=%async_computation.4 | async-start | bytes 983040 | tf_op jit(solution)/shard_map/reduce_scatter | solution.py:142
  20.3 15.3 %collective-permute-start = (bf16[1280,512]{1,0:T(8,128)(2,1)}, bf16[1280,512]{1,0:T(8,128)(2,1)}, u32[]{:S(2)}, u32[]{:S(2)}) collective-permute-start(bf16[1280,512]{1,0:T(8,128)(2,1)} %param.15), channel_id=1, source_target_pairs={{0,1},{1,0},{2,3},{3,2},{4,5},{5,4},{6,7},{7,6},{8,9},{9,8},{10,11... | collective-permute-start | bytes 3932168 | tf_op jit(solution)/shard_map/ppermute | solution.py:11
  21.1 4.1 %copy-start.30 = (s32[1280]{0:T(1024)S(1)}, s32[1280]{0:T(1024)}, u32[]{:S(2)}) copy-start(s32[1280]{0:T(1024)} %param.18) | copy-start | bytes 15364
  25.3 3.8 copy-start.5
  33.2 2.4 copy-start.7
  33.2 2.4 copy-start.9
  43.6 3.3 copy-start.28
  47.0 13.6 %copy-start.13 = (bf16[160,512]{1,0:T(8,128)(2,1)S(1)}, bf16[160,512]{1,0:T(8,128)(2,1)}, u32[]{:S(2)}) copy-start(bf16[160,512]{1,0:T(8,128)(2,1)} %param.14) | copy-start | bytes 491524
  58.1 279.1 %all-reduce.5.cloned.1.call-start = ((), (), s32[]{:S(2)}) async-start(), calls=%async_computation.6 | async-start | bytes 14680064 | tf_op jit(solution)/shard_map/psum | solution.py:179
  62.6 8.4 %copy-start.24 = (bf16[160,512]{1,0:T(8,128)(2,1)S(1)}, bf16[160,512]{1,0:T(8,128)(2,1)}, u32[]{:S(2)}) copy-start(bf16[160,512]{1,0:T(8,128)(2,1)} %param.16) | copy-start | bytes 491524
  62.6 8.4 %copy-start.32 = (f32[512]{0:T(512)S(1)}, f32[512]{0:T(512)}, u32[]{:S(2)}) copy-start(f32[512]{0:T(512)} %param.27) | copy-start | bytes 6148
  67.7 3.6 copy-start.33
  69.2 2.4 copy-start.26
  82.2 2.7 copy-start.2
  82.2 2.7 copy-start.4
  90.8 2.3 copy-start.27
  118.3 20.8 %all-to-all-start.1 = ((bf16[16,8,512]{2,1,0:T(8,128)(2,1)}), bf16[16,8,512]{2,1,0:T(8,128)(2,1)S(1)}, u32[]{:S(2)}, u32[]{:S(2)}) async-start(bf16[16,8,512]{2,1,0:T(8,128)(2,1)} %fusion.37), calls=%async_computation.2 | async-start | bytes 262144 | tf_op jit(solution)/shard_map/all_to_all | solution.py:166
  125.1 221.4 %reduce-scatter.5.cloned.1.call-start = ((), (), s32[]{:S(2)}) async-start(), calls=%async_computation.5 | async-start | bytes 983040 | tf_op jit(solution)/shard_map/reduce_scatter | solution.py:172
  141.6 243.1 %all-reduce.7.cloned.1.call-start = ((), (), s32[]{:S(2)}) async-start(), calls=%async_computation.7 | async-start | bytes 14680064 | tf_op jit(solution)/shard_map/psum | solution.py:178
  341.5 5.0 %copy-start.11 = (bf16[1024,512]{1,0:T(8,128)(2,1)S(1)}, bf16[1024,512]{1,0:T(8,128)(2,1)}, u32[]{:S(2)}) copy-start(bf16[1024,512]{1,0:T(8,128)(2,1)} %param.25) | copy-start | bytes 3145732
  384.7 3.6 copy-start.23
  384.7 4.6 %copy-start.12 = (f32[1024,512]{1,0:T(8,128)S(1)}, f32[1024,512]{1,0:T(8,128)}, u32[]{:S(2)}) copy-start(f32[1024,512]{1,0:T(8,128)} %get-tuple-element.28) | copy-start | bytes 6291460
  (18 other events, 27.9 us)
Sparse Core Ops, SparseCore 0:
  58.2 9.4 reduce-scatter.2
  100.8 236.3 all-reduce.4
  339.4 7.0 reduce-scatter.4
  349.1 35.5 all-reduce.6
